TPU v7x, 32 devices: a whole 2x2x4 slice. The times are simulated.
32 devices in a mesh: groups: 2 (over x), feat: 16 (over z, y, core).
Axes of the slice: x: 2, y: 2, z: 4, core: 2. Of those that a mesh axis runs over, the one named last changes fastest.
Arguments:
- inputs: bfloat16 [512, 2048], P('groups', 'feat'), parts along dimension 0, may hold values from -70 to 70
- norm_gains: float32 [2, 2048], P(None, 'feat'), may hold values from 0.1 to 1.9
- left_factors: bfloat16 [2, 16, 128, 128], P(None, 'feat'), may hold values from -0.5 to 0.5
- right_factors: bfloat16 [2, 128, 16, 16], P(None, 'feat'), may hold values from -1 to 1
- cotangent: bfloat16 [512, 2048], P('groups', 'feat'), parts along dimension 0, may hold values from -6 to 6
Outputs:
- output: bfloat16 [512, 2048], P('groups', 'feat'), parts along dimension 0
- grad_inputs: bfloat16 [512, 2048], P('groups', 'feat'), parts along dimension 0
- grad_gains: float32 [4, 2048], P('groups', 'feat'), parts along dimension 0
- grad_left: float32 [4, 16, 128, 128], P('groups', 'feat'), parts along dimension 0
- grad_right: float32 [4, 128, 16, 16], P('groups', 'feat'), parts along dimension 0
There are 2 independent parts, one for each index of `groups`. A program takes and returns all parts, laid end to end along the dimension named above; an argument that names none is the same for every part. Nothing has to cross between parts.
All inputs are finite; a program needn't handle non-finite values.
Results may differ from a plain program's by a relative error of at most 0.015.
Values may be sent and summed in bfloat16 or wider, within the bound.
A program may use at most 64 MiB of HBM per device.

v0:
```python
import functools

import jax
import jax.numpy as jnp
from jax import lax
from jax.experimental import pallas as pl
from jax.experimental.pallas import tpu as pltpu
from jax.sharding import PartitionSpec as P

BS = 128


epsilon = 1e-05
inv_root_two = 0.7071067811865476
inv_root_two_pi = 0.3989422804014327


def gelu_parts(pre):
    normal_cdf = 0.5 * (1.0 + jax.scipy.special.erf(pre * inv_root_two))
    normal_pdf = jnp.exp(-0.5 * pre * pre) * inv_root_two_pi
    return (pre * normal_cdf, normal_cdf + pre * normal_pdf)


def forward_layer(activation, gain, left, right):
    row_count = activation.shape[0]
    owned_blocks = left.shape[0]
    full_width = activation.shape[1] * lax.axis_size("feat")
    values = activation.astype(jnp.float32)
    totals = lax.psum(jnp.sum(values * values, axis=1, keepdims=True), "feat")
    inv_rms = lax.rsqrt(totals / full_width + epsilon)
    normed = (
        (values * inv_rms * gain[None, :]).astype(jnp.bfloat16).reshape(row_count, owned_blocks, BS)
    )
    first_mix = jnp.einsum("rbi,bij->rbj", normed, left, preferred_element_type=jnp.float32).astype(
        jnp.bfloat16
    )
    received = lax.all_to_all(first_mix, "feat", split_axis=2, concat_axis=1, tiled=True)
    pre_part = jnp.einsum("rbj,jbk->rjk", received, right, preferred_element_type=jnp.float32)
    gelu_value, gelu_slope = gelu_parts(pre_part)
    result = gelu_value.reshape(row_count, -1).astype(jnp.bfloat16)
    return (result, (values, inv_rms, normed, received, gelu_slope))


def backward_layer(upstream, stored, gain, left, right):
    values, inv_rms, normed, exchanged, gelu_slope = stored
    row_count = upstream.shape[0]
    owned_blocks = right.shape[0]
    block_count = right.shape[2]
    full_width = values.shape[1] * lax.axis_size("feat")
    grad_pre = (
        upstream.astype(jnp.float32).reshape(row_count, owned_blocks, block_count) * gelu_slope
    ).astype(jnp.bfloat16)
    grad_right = jnp.einsum("rbj,rjk->jbk", exchanged, grad_pre, preferred_element_type=jnp.float32)
    grad_mix = jnp.einsum(
        "rjk,jbk->rbj", grad_pre, right, preferred_element_type=jnp.float32
    ).astype(jnp.bfloat16)
    returned = lax.all_to_all(grad_mix, "feat", split_axis=1, concat_axis=2, tiled=True)
    grad_normed = jnp.einsum("rbj,bij->rbi", returned, left, preferred_element_type=jnp.float32)
    grad_left = jnp.einsum("rbi,rbj->bij", normed, returned, preferred_element_type=jnp.float32)
    grad_normed = grad_normed.reshape(row_count, -1)
    scaled = grad_normed * gain[None, :]
    inner_sum = lax.psum(jnp.sum(values * scaled, axis=1, keepdims=True), "feat")
    grad_in = (
        inv_rms * scaled - values * (inv_rms * inv_rms * inv_rms) * inner_sum / full_width
    ).astype(jnp.bfloat16)
    grad_gain = jnp.sum(grad_normed * values * inv_rms, axis=0)
    return (grad_in, grad_gain, grad_left, grad_right)


def body(inputs, norm_gains, left_factors, right_factors, cotangent):
    activation = inputs
    saved_all = []
    for layer_pos in range(2):
        activation, stored = forward_layer(
            activation, norm_gains[layer_pos], left_factors[layer_pos], right_factors[layer_pos]
        )
        saved_all.append(stored)
    upstream = cotangent
    gain_grads = [None, None]
    left_grads = [None, None]
    right_grads = [None, None]
    for layer_pos in (1, 0):
        upstream, grad_gain, grad_left, grad_right = backward_layer(
            upstream,
            saved_all[layer_pos],
            norm_gains[layer_pos],
            left_factors[layer_pos],
            right_factors[layer_pos],
        )
        gain_grads[layer_pos] = grad_gain
        left_grads[layer_pos] = grad_left
        right_grads[layer_pos] = grad_right
    return (
        activation,
        upstream,
        jnp.stack(gain_grads),
        jnp.stack(left_grads),
        jnp.stack(right_grads),
    )


def dot_plain(lhs, rhs):
    return lax.dot_general(lhs, rhs, (((1,), (0,)), ((), ())), preferred_element_type=jnp.float32)


def dot_left_transposed(lhs, rhs):
    return lax.dot_general(lhs, rhs, (((0,), (0,)), ((), ())), preferred_element_type=jnp.float32)


def dot_right_transposed(lhs, rhs):
    return lax.dot_general(lhs, rhs, (((1,), (1,)), ((), ())), preferred_element_type=jnp.float32)


def one_hot(condition):
    return jnp.where(condition, 1.0, 0.0).astype(jnp.bfloat16)


def iotas(rows, cols):
    return (
        lax.broadcasted_iota(jnp.int32, (rows, cols), 0),
        lax.broadcasted_iota(jnp.int32, (rows, cols), 1),
    )


def fused_kernel(
    peers,
    x_ref,
    gains_ref,
    left_ref,
    right_ref,
    cot_ref,
    out_ref,
    gin_ref,
    ggain_ref,
    gleft_ref,
    gright_ref,
    send_ref,
    recv_ref,
    stat_ref,
    stats_ref,
    send_sem,
    recv_sem,
    stat_send_sem,
    stat_recv_sem,
):
    rows, width = x_ref.shape
    half = rows // 2
    own_j, blocks, kk = right_ref.shape[1:]
    full_width = width * peers
    me = lax.axis_index("feat")

    barrier = pltpu.get_barrier_semaphore()
    for step in range(1, peers):
        pl.semaphore_signal(
            barrier,
            inc=1,
            device_id={"feat": lax.rem(me + step, peers)},
            device_id_type=pl.DeviceIdType.MESH,
        )

    def copies(turn, step):
        peer = lax.rem(me + step, peers)
        data = pltpu.make_async_remote_copy(
            src_ref=send_ref.at[turn, peer],
            dst_ref=recv_ref.at[turn, me],
            send_sem=send_sem.at[turn, step],
            recv_sem=recv_sem.at[turn, step],
            device_id={"feat": peer},
            device_id_type=pl.DeviceIdType.MESH,
        )
        stat = pltpu.make_async_remote_copy(
            src_ref=stat_ref.at[turn],
            dst_ref=stats_ref.at[turn, me],
            send_sem=stat_send_sem.at[turn, step],
            recv_sem=stat_recv_sem.at[turn, step],
            device_id={"feat": peer},
            device_id_type=pl.DeviceIdType.MESH,
        )
        return data, stat

    def start(turn, value, stat):
        slabs = value.reshape(peers, own_j, rows)
        slabs = jnp.concatenate([slabs[:, :, :half], slabs[:, :, half:]], axis=1)
        send_ref[turn] = slabs.astype(jnp.bfloat16)
        stat_ref[turn] = stat
        for step in range(1, peers):
            for copy in copies(turn, step):
                copy.start()
        recv_ref[turn, pl.ds(me, 1)] = send_ref[turn, pl.ds(me, 1)]
        stats_ref[turn, pl.ds(me, 1)] = stat_ref[turn].reshape(1, 1, rows)

    def finish(turn):
        for step in range(1, peers):
            for copy in copies(turn, step):
                copy.wait()
        got = recv_ref[turn].astype(jnp.float32)
        got = jnp.concatenate([got[:, :own_j], got[:, own_j:]], axis=2)
        got = got.reshape(peers * own_j, rows)
        return got, jnp.sum(stats_ref[turn], axis=0)

    row_id, col_id = iotas(width, width)
    gain_cols = [
        jnp.sum(
            jnp.where(row_id == col_id, gains_ref[layer : layer + 1, :], 0.0),
            axis=1,
            keepdims=True,
        )
        for layer in range(2)
    ]
    lefts = [left_ref[layer, 0] for layer in range(2)]
    gained = [
        (lefts[layer].astype(jnp.float32) * gain_cols[layer]).astype(jnp.bfloat16)
        for layer in range(2)
    ]
    act0 = x_ref[...].astype(jnp.float32).T
    mixed0 = dot_left_transposed(gained[0], act0.astype(jnp.bfloat16))
    square0 = jnp.sum(act0 * act0, axis=0, keepdims=True)

    pl.semaphore_wait(barrier, peers - 1)
    start(0, mixed0, square0)

    pick_r, pick_c = iotas(width, kk)
    pick_k = one_hot(pick_r % kk == pick_c)
    same_j = row_id // kk == col_id // blocks
    spread = one_hot(row_id % blocks == col_id // own_j)
    on_j = row_id // kk == col_id % own_j
    right_mats = []
    for layer in range(2):
        flat = right_ref[layer].reshape(own_j * blocks, kk)
        by_k = jnp.where(same_j, dot_right_transposed(pick_k, flat), 0.0).astype(jnp.bfloat16)
        mat = jnp.where(on_j, dot_plain(by_k, spread), 0.0).astype(jnp.bfloat16)
        right_mats.append(mat)
    reorder = one_hot((col_id // own_j == row_id % blocks) & (col_id % own_j == row_id // blocks))
    keep_j = row_id // blocks == col_id // kk
    cot = cot_ref[...].astype(jnp.float32).T

    def forward(turn, layer):
        got, total = finish(turn)
        inv_rms = lax.rsqrt(total / full_width + epsilon)
        raw = dot_plain(right_mats[layer], got.astype(jnp.bfloat16))
        pre = raw * inv_rms
        cdf = 0.5 * (1.0 + lax.erf(pre * inv_root_two))
        return got, inv_rms, raw, pre, cdf

    def slope_of(pre, cdf):
        return cdf + pre * (jnp.exp(-0.5 * pre * pre) * inv_root_two_pi)

    def right_grad(layer, got, inv_rms, grad_pre):
        exchanged = (got * inv_rms).astype(jnp.bfloat16)
        ordered = dot_plain(reorder, exchanged).astype(jnp.bfloat16)
        prods = dot_right_transposed(ordered, grad_pre)
        prods = jnp.where(keep_j, prods, 0.0)
        shift = width // 2
        while shift >= kk:
            prods = prods + pltpu.roll(prods, shift, 1)
            shift //= 2
        gright_ref[layer] = prods[:, :kk].reshape(own_j, blocks, kk)

    def backward(turn, layer, act, inv_rms):
        got, inner = finish(turn)
        got = got.astype(jnp.bfloat16)
        grad_normed = dot_plain(lefts[layer], got)
        scaled = grad_normed * gain_cols[layer]
        upstream = inv_rms * scaled - act * (inv_rms * inv_rms * inv_rms) * inner / full_width
        return got, grad_normed, upstream

    def left_grads(layer, act, inv_rms, got, grad_normed):
        centred = act * inv_rms
        normed = (centred * gain_cols[layer]).astype(jnp.bfloat16)
        gleft_ref[layer, 0] = dot_right_transposed(normed, got)
        column = jnp.sum(grad_normed * centred, axis=1, keepdims=True)
        ggain_ref[layer : layer + 1, :] = jnp.sum(
            jnp.where(row_id == col_id, column, 0.0), axis=0, keepdims=True
        )

    got1, inv1, raw1, pre1, cdf1 = forward(0, 0)
    act1_low = (pre1 * cdf1).astype(jnp.bfloat16)
    act1 = act1_low.astype(jnp.float32)
    start(1, dot_left_transposed(gained[1], act1_low), jnp.sum(act1 * act1, axis=0, keepdims=True))
    slope1 = slope_of(pre1, cdf1)
    inv0 = inv1

    got2, inv2, raw2, pre2, cdf2 = forward(1, 1)
    grad_pre2 = (cot * slope_of(pre2, cdf2)).astype(jnp.bfloat16)
    start(
        2,
        dot_left_transposed(right_mats[1], grad_pre2),
        jnp.sum(grad_pre2.astype(jnp.float32) * raw2, axis=0, keepdims=True),
    )
    out_ref[...] = (pre2 * cdf2).T.astype(out_ref.dtype)
    right_grad(1, got2, inv2, grad_pre2)

    back2, grad_normed2, up1 = backward(2, 1, act1, inv2)
    up1 = up1.astype(jnp.bfloat16).astype(jnp.float32)
    grad_pre1 = (up1 * slope1).astype(jnp.bfloat16)
    start(
        3,
        dot_left_transposed(right_mats[0], grad_pre1),
        jnp.sum(grad_pre1.astype(jnp.float32) * raw1, axis=0, keepdims=True),
    )
    right_grad(0, got1, inv0, grad_pre1)
    left_grads(1, act1, inv2, back2, grad_normed2)

    back1, grad_normed1, up0 = backward(3, 0, act0, inv0)
    gin_ref[...] = up0.T.astype(gin_ref.dtype)
    left_grads(0, act0, inv0, back1, grad_normed1)


def device_body(peers, inputs, norm_gains, left_factors, right_factors, cotangent):
    rows, width = inputs.shape
    own_j, blocks, kk = right_factors.shape[1:]
    args = (inputs, norm_gains, left_factors, right_factors, cotangent)
    fits = (
        rows == 2 * BS
        and width == BS
        and left_factors.shape[1] == 1
        and blocks == peers
        and own_j % 8 == 0
        and kk % 8 == 0
    )
    if not fits:
        return body(*args)
    half = rows // 2
    turns = 4
    vmem = pl.BlockSpec(memory_space=pltpu.VMEM)
    return pl.pallas_call(
        functools.partial(fused_kernel, peers),
        out_shape=(
            jax.ShapeDtypeStruct((rows, width), jnp.bfloat16),
            jax.ShapeDtypeStruct((rows, width), jnp.bfloat16),
            jax.ShapeDtypeStruct(norm_gains.shape, jnp.float32),
            jax.ShapeDtypeStruct(left_factors.shape, jnp.float32),
            jax.ShapeDtypeStruct(right_factors.shape, jnp.float32),
        ),
        in_specs=[vmem] * 5,
        out_specs=(vmem,) * 5,
        scratch_shapes=[
            pltpu.VMEM((turns, peers, 2 * own_j, half), jnp.bfloat16),
            pltpu.VMEM((turns, peers, 2 * own_j, half), jnp.bfloat16),
            pltpu.VMEM((turns, 1, rows), jnp.float32),
            pltpu.VMEM((turns, peers, 1, rows), jnp.float32),
            pltpu.SemaphoreType.DMA((turns, peers)),
            pltpu.SemaphoreType.DMA((turns, peers)),
            pltpu.SemaphoreType.DMA((turns, peers)),
            pltpu.SemaphoreType.DMA((turns, peers)),
        ],
        compiler_params=pltpu.CompilerParams(collective_id=0, has_side_effects=True),
    )(*args)


def solution(mesh):
    return jax.shard_map(
        functools.partial(device_body, mesh.shape["feat"]),
        mesh=mesh,
        in_specs=(
            P("groups", "feat"),
            P(None, "feat"),
            P(None, "feat", None, None),
            P(None, "feat", None, None),
            P("groups", "feat"),
        ),
        out_specs=(
            P("groups", "feat"),
            P("groups", "feat"),
            P("groups", "feat"),
            P("groups", "feat", None, None),
            P("groups", "feat", None, None),
        ),
        check_vma=False,
    )
```

profile of v0, /device:TPU:0, one launch (start us, length us, event | category | flops | bytes accessed | tf_op | source)
XLA Modules:
  0.0 33.8 jit_solution(18092407884166430273)
XLA Ops:
  0.6 28.7 %shard_map.92 = (bf16[256,128]{1,0:T(8,128)(2,1)}, bf16[256,128]{1,0:T(8,128)(2,1)}, f32[2,128]{1,0:T(2,128)}, f32[2,1,128,128]{3,2,1,0:T(8,128)}, f32[2,8,16,16]{3,2,1,0:T(8,128)}) custom-call(bf16[256,128]{1,0:T(8,128)(2,1)} %x_ref.1, f32[2,128]{1,0:T(2,128)} %gains_ref.1, bf16[2,1,128,128]{3,2,1,0:T(8,128)(2,1)} %left_ref.1, ...), custom_call_target="tpu_custom_call" | custom-call | tf_op jit(solution)/shard_map/pallas_call | solution.py:326
  29.4 0.0 copy-start.2
  29.4 0.0 copy-start.1
  29.4 1.5 %copy.15 = bf16[256,128]{1,0:T(8,128)(2,1)} copy(bf16[256,128]{1,0:T(8,128)(2,1)} %get-tuple-element.10) | data formatting | bytes 131072
  30.9 0.0 copy-done.2
  30.9 0.0 copy-start.3
  30.9 0.6 %copy.16 = bf16[256,128]{1,0:T(8,128)(2,1)} copy(bf16[256,128]{1,0:T(8,128)(2,1)S(1)} %copy-done.2) | data formatting | bytes 131072
  31.5 0.0 copy-done.3
  31.6 0.6 %copy.17 = f32[2,128]{1,0:T(2,128)} copy(f32[2,128]{1,0:T(2,128)S(1)} %copy-done.3) | data formatting | bytes 2048
  32.2 0.0 copy-done.1
  32.2 0.0 copy-start
  32.2 0.7 %copy.18 = f32[2,1,128,128]{3,2,1,0:T(8,128)} copy(f32[2,1,128,128]{3,2,1,0:T(8,128)S(1)} %copy-done.1) | data formatting | bytes 262144
  32.8 0.3 copy-done
  33.1 0.7 %copy.19 = f32[2,8,16,16]{3,2,1,0:T(8,128)} copy(f32[2,8,16,16]{3,2,1,0:T(8,128)S(1)} %copy-done) | data formatting | bytes 32768
Async XLA Ops:
  29.4 1.5 %copy-start.2 = (bf16[256,128]{1,0:T(8,128)(2,1)S(1)}, bf16[256,128]{1,0:T(8,128)(2,1)}, u32[]{:S(2)}) copy-start(bf16[256,128]{1,0:T(8,128)(2,1)} %get-tuple-element.11) | copy-start | bytes 196612
  29.4 2.8 %copy-start.1 = (f32[2,1,128,128]{3,2,1,0:T(8,128)S(1)}, f32[2,1,128,128]{3,2,1,0:T(8,128)}, u32[]{:S(2)}) copy-start(f32[2,1,128,128]{3,2,1,0:T(8,128)} %get-tuple-element.13) | copy-start | bytes 393220
  30.9 0.7 %copy-start.3 = (f32[2,128]{1,0:T(2,128)S(1)}, f32[2,128]{1,0:T(2,128)}, u32[]{:S(2)}) copy-start(f32[2,128]{1,0:T(2,128)} %get-tuple-element.12) | copy-start | bytes 3076
  32.2 1.0 %copy-start = (f32[2,8,16,16]{3,2,1,0:T(8,128)S(1)}, f32[2,8,16,16]{3,2,1,0:T(8,128)}, u32[]{:S(2)}) copy-start(f32[2,8,16,16]{3,2,1,0:T(8,128)} %get-tuple-element.14) | copy-start | bytes 49156
where the time goes:
time: 34 us; the launch traced here: 33.8 us
  Pallas kernels  28.7 us (84%)
  local copies, waits for them, and re-layouts  4.37 us (13%)
  between operations  0.66 us (2%)
    pallas_call x1, Pallas kernels, device_body(): pl.pallas_call(functools.partial(fused_kernel, peers), out_shape=(jax.Sha...  28.7 us
    unnamed x13, local copies, waits for them, and re-layouts  4.37 us

commit v1 on v0

--- a/solution.py
+++ b/solution.py
@@ -124,16 +124,22 @@
 
 def fused_kernel(
     peers,
+    x_any,
+    gains_any,
+    left_any,
+    right_any,
+    cot_any,
+    out_ref,
+    gin_ref,
+    ggain_ref,
+    gleft_ref,
+    gright_ref,
     x_ref,
     gains_ref,
     left_ref,
     right_ref,
     cot_ref,
-    out_ref,
-    gin_ref,
-    ggain_ref,
-    gleft_ref,
-    gright_ref,
+    load_sem,
     send_ref,
     recv_ref,
     stat_ref,
@@ -143,6 +149,20 @@
     stat_send_sem,
     stat_recv_sem,
 ):
+    loads = [
+        pltpu.make_async_copy(source, target, load_sem.at[place])
+        for place, (source, target) in enumerate(
+            (
+                (x_any, x_ref),
+                (gains_any, gains_ref),
+                (left_any, left_ref),
+                (right_any, right_ref),
+                (cot_any, cot_ref),
+            )
+        )
+    ]
+    for load in loads:
+        load.start()
     rows, width = x_ref.shape
     half = rows // 2
     own_j, blocks, kk = right_ref.shape[1:]
@@ -157,6 +177,9 @@
             device_id={"feat": lax.rem(me + step, peers)},
             device_id_type=pl.DeviceIdType.MESH,
         )
+
+    for load in loads:
+        load.wait()
 
     def copies(turn, step):
         peer = lax.rem(me + step, peers)
@@ -183,7 +206,7 @@
         slabs = jnp.concatenate([slabs[:, :, :half], slabs[:, :, half:]], axis=1)
         send_ref[turn] = slabs.astype(jnp.bfloat16)
         stat_ref[turn] = stat
-        for step in range(1, peers):
+        for step in sorted(range(1, peers), key=lambda gap: abs(gap - peers // 2)):
             for copy in copies(turn, step):
                 copy.start()
         recv_ref[turn, pl.ds(me, 1)] = send_ref[turn, pl.ds(me, 1)]
@@ -306,6 +329,18 @@
     left_grads(0, act0, inv0, back1, grad_normed1)
 
 
+def write_kernel(*refs):
+    sources, targets, sem = refs[:5], refs[5:10], refs[10]
+    writes = [
+        pltpu.make_async_copy(source, target, sem.at[place])
+        for place, (source, target) in enumerate(zip(sources, targets))
+    ]
+    for write in writes:
+        write.start()
+    for write in writes:
+        write.wait()
+
+
 def device_body(peers, inputs, norm_gains, left_factors, right_factors, cotangent):
     rows, width = inputs.shape
     own_j, blocks, kk = right_factors.shape[1:]
@@ -323,18 +358,22 @@
     half = rows // 2
     turns = 4
     vmem = pl.BlockSpec(memory_space=pltpu.VMEM)
-    return pl.pallas_call(
+    in_hbm = pl.BlockSpec(memory_space=pltpu.HBM)
+    shapes = (
+        ((rows, width), jnp.bfloat16),
+        ((rows, width), jnp.bfloat16),
+        (norm_gains.shape, jnp.float32),
+        (left_factors.shape, jnp.float32),
+        (right_factors.shape, jnp.float32),
+    )
+    results = pl.pallas_call(
         functools.partial(fused_kernel, peers),
-        out_shape=(
-            jax.ShapeDtypeStruct((rows, width), jnp.bfloat16),
-            jax.ShapeDtypeStruct((rows, width), jnp.bfloat16),
-            jax.ShapeDtypeStruct(norm_gains.shape, jnp.float32),
-            jax.ShapeDtypeStruct(left_factors.shape, jnp.float32),
-            jax.ShapeDtypeStruct(right_factors.shape, jnp.float32),
-        ),
-        in_specs=[vmem] * 5,
+        out_shape=tuple(pltpu.VMEM(*shape) for shape in shapes),
+        in_specs=[in_hbm] * 5,
         out_specs=(vmem,) * 5,
-        scratch_shapes=[
+        scratch_shapes=[pltpu.VMEM(arg.shape, arg.dtype) for arg in args]
+        + [
+            pltpu.SemaphoreType.DMA((len(args),)),
             pltpu.VMEM((turns, peers, 2 * own_j, half), jnp.bfloat16),
             pltpu.VMEM((turns, peers, 2 * own_j, half), jnp.bfloat16),
             pltpu.VMEM((turns, 1, rows), jnp.float32),
@@ -344,8 +383,18 @@
             pltpu.SemaphoreType.DMA((turns, peers)),
             pltpu.SemaphoreType.DMA((turns, peers)),
         ],
-        compiler_params=pltpu.CompilerParams(collective_id=0, has_side_effects=True),
-    )(*args)
+        compiler_params=pltpu.CompilerParams(
+            collective_id=0, has_side_effects=True, vmem_limit_bytes=16 * 2**20
+        ),
+    )(*(pltpu.with_memory_space_constraint(arg, pltpu.HBM) for arg in args))
+    return pl.pallas_call(
+        write_kernel,
+        out_shape=tuple(pltpu.HBM(*shape) for shape in shapes),
+        in_specs=[vmem] * 5,
+        out_specs=(in_hbm,) * 5,
+        scratch_shapes=[pltpu.SemaphoreType.DMA((5,))],
+        compiler_params=pltpu.CompilerParams(vmem_limit_bytes=4 * 2**20),
+    )(*(pltpu.with_memory_space_constraint(result, pltpu.VMEM) for result in results))
 
 
 def solution(mesh):

time: 34 us -> 30 us (0.88)
  local copies, waits for them, and re-layouts: 4.37 us -> 0 us
  Pallas kernels: 28.7 us -> 29.2 us
    unnamed x13 -> x0, local copies, waits for them, and re-layouts: 4.37 us -> none
    pallas_call x1 -> x2, Pallas kernels: 28.7 us -> 29.2 us  [the longest x1 28.4 us: device_body(): pl.pallas_call(functools.partial(fused_kernel, peers), out_shape=tuple((p...]
where the time goes in v1:
time: 30 us; the launch traced here: 29.8 us
  Pallas kernels  29.2 us (97%)
  between operations  0.64 us (2%)
    pallas_call x1, Pallas kernels, device_body(): pl.pallas_call(functools.partial(fused_kernel, peers), out_shape=tuple((p...  28.4 us
    pallas_call x1, Pallas kernels, device_body(): pl.pallas_call(write_kernel, out_shape=tuple((pltpu.HBM(*shape) for shape...  0.79 us

profile of v1, /device:TPU:0, one launch (start us, length us, event | category | flops | bytes accessed | tf_op | source)
XLA Modules:
  0.0 29.8 jit_solution(8878393207614799592)
XLA Ops:
  0.6 28.4 %shard_map.92 = (bf16[256,128]{1,0:T(8,128)(2,1)S(1)}, bf16[256,128]{1,0:T(8,128)(2,1)S(1)}, f32[2,128]{1,0:T(2,128)S(1)}, f32[2,1,128,128]{3,2,1,0:T(8,128)S(1)}, f32[2,8,16,16]{3,2,1,0:T(8,128)S(1)}) custom-call(bf16[256,128]{1,0:T(8,128)(2,1)} %x_any.1, f32[2,128]{1,0:T(2,128)} %gains_any.1, bf16[2,1,128,128]{3,2,1,0:T(8,128)(2,1)} %left_any.1, ...), custom_call_target="tpu_custom_call" | custom-call | tf_op jit(solution)/shard_map/pallas_call | solution.py:369
  29.0 0.8 %shard_map.93 = (bf16[256,128]{1,0:T(8,128)(2,1)}, bf16[256,128]{1,0:T(8,128)(2,1)}, f32[2,128]{1,0:T(2,128)}, f32[2,1,128,128]{3,2,1,0:T(8,128)}, f32[2,8,16,16]{3,2,1,0:T(8,128)}) custom-call(bf16[256,128]{1,0:T(8,128)(2,1)S(1)} %get-tuple-element.10.refs_0_, bf16[256,128]{1,0:T(8,128)(2,1)S(1)} %get-tuple-element.11.refs_1_, ...), custom_call_target="tpu_custom_call" | custom-call | tf_op jit(solution)/shard_map/pallas_call | solution.py:390

commit v2 on v1

--- a/solution.py
+++ b/solution.py
@@ -178,11 +178,16 @@
             device_id_type=pl.DeviceIdType.MESH,
         )
 
-    for load in loads:
+    for load in loads[:3]:
         load.wait()
 
+    flips = [bit * (1 - 2 * (me // bit % 2)) for bit in (1 << p for p in range(peers.bit_length() - 1))]
+
+    def partner(step):
+        return me + sum(flip for place, flip in enumerate(flips) if step >> place & 1)
+
     def copies(turn, step):
-        peer = lax.rem(me + step, peers)
+        peer = partner(step)
         data = pltpu.make_async_remote_copy(
             src_ref=send_ref.at[turn, peer],
             dst_ref=recv_ref.at[turn, me],
@@ -201,16 +206,22 @@
         )
         return data, stat
 
-    def start(turn, value, stat):
+    def stage(turn, value, stat):
         slabs = value.reshape(peers, own_j, rows)
         slabs = jnp.concatenate([slabs[:, :, :half], slabs[:, :, half:]], axis=1)
         send_ref[turn] = slabs.astype(jnp.bfloat16)
         stat_ref[turn] = stat
-        for step in sorted(range(1, peers), key=lambda gap: abs(gap - peers // 2)):
+
+    def launch(turn):
+        for step in range(peers - 1, 0, -1):
             for copy in copies(turn, step):
                 copy.start()
         recv_ref[turn, pl.ds(me, 1)] = send_ref[turn, pl.ds(me, 1)]
         stats_ref[turn, pl.ds(me, 1)] = stat_ref[turn].reshape(1, 1, rows)
+
+    def start(turn, value, stat):
+        stage(turn, value, stat)
+        launch(turn)
 
     def finish(turn):
         for step in range(1, peers):
@@ -239,8 +250,12 @@
     mixed0 = dot_left_transposed(gained[0], act0.astype(jnp.bfloat16))
     square0 = jnp.sum(act0 * act0, axis=0, keepdims=True)
 
+    stage(0, mixed0, square0)
     pl.semaphore_wait(barrier, peers - 1)
-    start(0, mixed0, square0)
+    launch(0)
+
+    for load in loads[3:]:
+        load.wait()
 
     pick_r, pick_c = iotas(width, kk)
     pick_k = one_hot(pick_r % kk == pick_c)
@@ -279,19 +294,24 @@
             shift //= 2
         gright_ref[layer] = prods[:, :kk].reshape(own_j, blocks, kk)
 
-    def backward(turn, layer, act, inv_rms):
+    def backward_factors(layer, act, inv_rms):
+        centred = act * inv_rms
+        return (
+            inv_rms * gain_cols[layer],
+            centred * (inv_rms * inv_rms / full_width),
+            centred,
+            (centred * gain_cols[layer]).astype(jnp.bfloat16),
+        )
+
+    def backward(turn, layer, factors):
         got, inner = finish(turn)
         got = got.astype(jnp.bfloat16)
         grad_normed = dot_plain(lefts[layer], got)
-        scaled = grad_normed * gain_cols[layer]
-        upstream = inv_rms * scaled - act * (inv_rms * inv_rms * inv_rms) * inner / full_width
-        return got, grad_normed, upstream
-
-    def left_grads(layer, act, inv_rms, got, grad_normed):
-        centred = act * inv_rms
-        normed = (centred * gain_cols[layer]).astype(jnp.bfloat16)
-        gleft_ref[layer, 0] = dot_right_transposed(normed, got)
-        column = jnp.sum(grad_normed * centred, axis=1, keepdims=True)
+        return got, grad_normed, factors[0] * grad_normed - factors[1] * inner
+
+    def left_grads(layer, factors, got, grad_normed):
+        gleft_ref[layer, 0] = dot_right_transposed(factors[3], got)
+        column = jnp.sum(grad_normed * factors[2], axis=1, keepdims=True)
         ggain_ref[layer : layer + 1, :] = jnp.sum(
             jnp.where(row_id == col_id, column, 0.0), axis=0, keepdims=True
         )
@@ -313,7 +333,8 @@
     out_ref[...] = (pre2 * cdf2).T.astype(out_ref.dtype)
     right_grad(1, got2, inv2, grad_pre2)
 
-    back2, grad_normed2, up1 = backward(2, 1, act1, inv2)
+    factors2 = backward_factors(1, act1, inv2)
+    back2, grad_normed2, up1 = backward(2, 1, factors2)
     up1 = up1.astype(jnp.bfloat16).astype(jnp.float32)
     grad_pre1 = (up1 * slope1).astype(jnp.bfloat16)
     start(
@@ -322,11 +343,12 @@
         jnp.sum(grad_pre1.astype(jnp.float32) * raw1, axis=0, keepdims=True),
     )
     right_grad(0, got1, inv0, grad_pre1)
-    left_grads(1, act1, inv2, back2, grad_normed2)
-
-    back1, grad_normed1, up0 = backward(3, 0, act0, inv0)
-    gin_ref[...] = up0.T.astype(gin_ref.dtype)
-    left_grads(0, act0, inv0, back1, grad_normed1)
+    left_grads(1, factors2, back2, grad_normed2)
+
+    factors1 = backward_factors(0, act0, inv0)
+    back1, grad_normed1, up0 = backward(3, 0, factors1)
+    gin_ref[...] = up0.astype(gin_ref.dtype).T
+    left_grads(0, factors1, back1, grad_normed1)
 
 
 def write_kernel(*refs):
@@ -350,6 +372,7 @@
         and width == BS
         and left_factors.shape[1] == 1
         and blocks == peers
+        and peers & (peers - 1) == 0
         and own_j % 8 == 0
         and kk % 8 == 0
     )

time: 30 us -> 27.6 us (0.920)
  Pallas kernels: 29.2 us -> 26.8 us
    pallas_call x1, Pallas kernels: 28.4 us -> 26 us  [device_body(): pl.pallas_call(functools.partial(fused_kernel, peers), out_shape=tuple((p...]
where the time goes in v2:
time: 27.6 us; the launch traced here: 27.4 us
  Pallas kernels  26.8 us (97%)
  between operations  0.64 us (2%)
    pallas_call x1, Pallas kernels, device_body(): pl.pallas_call(functools.partial(fused_kernel, peers), out_shape=tuple((p...  26 us
    pallas_call x1, Pallas kernels, device_body(): pl.pallas_call(write_kernel, out_shape=tuple((pltpu.HBM(*shape) for shape...  0.79 us

profile of v2, /device:TPU:0, one launch (start us, length us, event | category | flops | bytes accessed | tf_op | source)
XLA Modules:
  0.0 27.4 jit_solution(12270562143497953352)
XLA Ops:
  0.6 26.0 %shard_map.92 = (bf16[256,128]{1,0:T(8,128)(2,1)S(1)}, bf16[256,128]{1,0:T(8,128)(2,1)S(1)}, f32[2,128]{1,0:T(2,128)S(1)}, f32[2,1,128,128]{3,2,1,0:T(8,128)S(1)}, f32[2,8,16,16]{3,2,1,0:T(8,128)S(1)}) custom-call(bf16[256,128]{1,0:T(8,128)(2,1)} %x_any.1, f32[2,128]{1,0:T(2,128)} %gains_any.1, bf16[2,1,128,128]{3,2,1,0:T(8,128)(2,1)} %left_any.1, ...), custom_call_target="tpu_custom_call" | custom-call | tf_op jit(solution)/shard_map/pallas_call | solution.py:392
  26.6 0.8 %shard_map.93 = (bf16[256,128]{1,0:T(8,128)(2,1)}, bf16[256,128]{1,0:T(8,128)(2,1)}, f32[2,128]{1,0:T(2,128)}, f32[2,1,128,128]{3,2,1,0:T(8,128)}, f32[2,8,16,16]{3,2,1,0:T(8,128)}) custom-call(bf16[256,128]{1,0:T(8,128)(2,1)S(1)} %get-tuple-element.10.refs_0_, bf16[256,128]{1,0:T(8,128)(2,1)S(1)} %get-tuple-element.11.refs_1_, ...), custom_call_target="tpu_custom_call" | custom-call | tf_op jit(solution)/shard_map/pallas_call | solution.py:413

commit v3 on v2

--- a/solution.py
+++ b/solution.py
@@ -161,30 +161,30 @@
             )
         )
     ]
-    for load in loads:
-        load.start()
     rows, width = x_ref.shape
     half = rows // 2
     own_j, blocks, kk = right_ref.shape[1:]
     full_width = width * peers
     me = lax.axis_index("feat")
 
+    flips = [bit * (1 - 2 * (me // bit % 2)) for bit in (1 << p for p in range(peers.bit_length() - 1))]
+
+    def partner(step):
+        return me + sum(flip for place, flip in enumerate(flips) if step >> place & 1)
+
     barrier = pltpu.get_barrier_semaphore()
-    for step in range(1, peers):
+    for step in range(peers - 1, 0, -1):
         pl.semaphore_signal(
             barrier,
             inc=1,
-            device_id={"feat": lax.rem(me + step, peers)},
+            device_id={"feat": partner(step)},
             device_id_type=pl.DeviceIdType.MESH,
         )
 
+    for load in loads:
+        load.start()
     for load in loads[:3]:
         load.wait()
-
-    flips = [bit * (1 - 2 * (me // bit % 2)) for bit in (1 << p for p in range(peers.bit_length() - 1))]
-
-    def partner(step):
-        return me + sum(flip for place, flip in enumerate(flips) if step >> place & 1)
 
     def copies(turn, step):
         peer = partner(step)
@@ -214,7 +214,7 @@
 
     def launch(turn):
         for step in range(peers - 1, 0, -1):
-            for copy in copies(turn, step):
+            for copy in copies(turn, step)[::-1]:
                 copy.start()
         recv_ref[turn, pl.ds(me, 1)] = send_ref[turn, pl.ds(me, 1)]
         stats_ref[turn, pl.ds(me, 1)] = stat_ref[turn].reshape(1, 1, rows)
@@ -311,10 +311,12 @@
 
     def left_grads(layer, factors, got, grad_normed):
         gleft_ref[layer, 0] = dot_right_transposed(factors[3], got)
-        column = jnp.sum(grad_normed * factors[2], axis=1, keepdims=True)
-        ggain_ref[layer : layer + 1, :] = jnp.sum(
-            jnp.where(row_id == col_id, column, 0.0), axis=0, keepdims=True
-        )
+        prods = grad_normed * factors[2]
+        high = prods.astype(jnp.bfloat16)
+        low = (prods - high.astype(jnp.float32)).astype(jnp.bfloat16)
+        ones = jnp.ones((8, rows), jnp.bfloat16)
+        sums = dot_right_transposed(ones, high) + dot_right_transposed(ones, low)
+        ggain_ref[layer : layer + 1, :] = sums[:1]
 
     got1, inv1, raw1, pre1, cdf1 = forward(0, 0)
     act1_low = (pre1 * cdf1).astype(jnp.bfloat16)

time: 27.6 us -> 27.5 us (level)
  no operation moved by 1% of the time
where the time goes in v3:
time: 27.5 us; the launch traced here: 27.4 us
  Pallas kernels  26.7 us (97%)
  between operations  0.64 us (2%)
    pallas_call x1, Pallas kernels, device_body(): pl.pallas_call(functools.partial(fused_kernel, peers), out_shape=tuple((p...  25.9 us
    pallas_call x1, Pallas kernels, device_body(): pl.pallas_call(write_kernel, out_shape=tuple((pltpu.HBM(*shape) for shape...  0.79 us

profile of v3, /device:TPU:0, one launch (start us, length us, event | category | flops | bytes accessed | tf_op | source)
XLA Modules:
  0.0 27.4 jit_solution(3693704173608187929)
XLA Ops:
  0.6 25.9 %shard_map.92 = (bf16[256,128]{1,0:T(8,128)(2,1)S(1)}, bf16[256,128]{1,0:T(8,128)(2,1)S(1)}, f32[2,128]{1,0:T(2,128)S(1)}, f32[2,1,128,128]{3,2,1,0:T(8,128)S(1)}, f32[2,8,16,16]{3,2,1,0:T(8,128)S(1)}) custom-call(bf16[256,128]{1,0:T(8,128)(2,1)} %x_any.1, f32[2,128]{1,0:T(2,128)} %gains_any.1, bf16[2,1,128,128]{3,2,1,0:T(8,128)(2,1)} %left_any.1, ...), custom_call_target="tpu_custom_call" | custom-call | tf_op jit(solution)/shard_map/pallas_call | solution.py:394
  26.6 0.8 %shard_map.93 = (bf16[256,128]{1,0:T(8,128)(2,1)}, bf16[256,128]{1,0:T(8,128)(2,1)}, f32[2,128]{1,0:T(2,128)}, f32[2,1,128,128]{3,2,1,0:T(8,128)}, f32[2,8,16,16]{3,2,1,0:T(8,128)}) custom-call(bf16[256,128]{1,0:T(8,128)(2,1)S(1)} %get-tuple-element.10.refs_0_, bf16[256,128]{1,0:T(8,128)(2,1)S(1)} %get-tuple-element.11.refs_1_, ...), custom_call_target="tpu_custom_call" | custom-call | tf_op jit(solution)/shard_map/pallas_call | solution.py:415
